TPU v7x, 512 devices: a whole 4x4x16 slice. The times are simulated.
512 devices in a mesh: dp: 32 (over x, z_hi, core), tensor: 16 (over y, z_lo).
Axes of the slice: x: 4, y: 4, z: 16 (z_hi: 4, z_lo: 4; z = z_hi * 4 + z_lo), core: 2. Of those that a mesh axis runs over, the one named last changes fastest.
Arguments:
- rm_hidden: bfloat16 [32, 1024, 3584], P('dp', 'tensor'), may hold values from -6 to 6
- rm_cotangent: bfloat16 [32, 1024, 3584], P('dp', 'tensor'), may hold values from -6 to 6
- rm_gain: float32 [3584], replicated, may hold values from 0.25 to 1.75
- rewards: float32 [32], P('dp'), may hold values from 0.25 to 8, as said below
- visual_pos: int32 [32, 512], P('dp', 'tensor'), may hold values from 0 to 1023, as said below
- bridge: bfloat16 [3584, 2048], P(None, 'tensor'), may hold values from -0.09375 to 0.09375
- img_query: bfloat16 [32, 2048, 2048], P('dp', 'tensor'), may hold values from -8 to 8
- img_key: bfloat16 [32, 2048, 2048], P('dp', 'tensor'), may hold values from -8 to 8
- img_value: bfloat16 [32, 2048, 2048], P('dp', 'tensor'), may hold values from -6 to 6
Outputs:
- grad_query: bfloat16 [32, 2048, 2048], P('dp', 'tensor')
- grad_key: bfloat16 [32, 2048, 2048], P('dp', 'tensor')
- grad_value: bfloat16 [32, 2048, 2048], P('dp', 'tensor')
Inputs may be any that keep to these rules, and one draw needn't show every extreme that they name: `visual_pos`: strictly increasing in each sample; rows 64 * t to 64 * t + 63 of a reward sequence hold exactly 32 visual tokens, for every t. `rewards`: positive.
All inputs are finite; a program needn't handle non-finite values.
Results may differ from a plain program's by a relative error of at most 0.0082.
Values may be sent and summed in bfloat16 or wider, within the bound.
A program may use at most 64 MiB of HBM per device.

v0:
```python
import functools
import jax
import jax.numpy as jnp
from jax import lax
from jax.sharding import Mesh
from jax.sharding import PartitionSpec as P

HD = 128
GW = 64
DP = ("dp_0", "dp_1", "dp_2")


def one_axis_at_a_time(array, axes):
    return functools.reduce(lax.psum, axes, array)


def norm_backward(hidden, cotangent, gain):
    hidden_f = hidden.astype(jnp.float32)
    scaled_cot = cotangent.astype(jnp.float32) * gain
    inv_rms = lax.rsqrt(jnp.mean(hidden_f * hidden_f, axis=-1, keepdims=True) + 1e-06)
    mixed = jnp.mean(hidden_f * scaled_cot, axis=-1, keepdims=True)
    return (inv_rms * scaled_cot - hidden_f * inv_rms * inv_rms * inv_rms * mixed).astype(
        jnp.bfloat16
    )


def upsample(handed):
    half_width = GW // 2
    grid_rows = handed.reshape(handed.shape[0] // half_width, half_width, handed.shape[1])
    grid_rows = jnp.repeat(jnp.repeat(grid_rows, 2, axis=0), 2, axis=1)
    return grid_rows.reshape(-1, handed.shape[1])


def attend_back(query_rows, key_rows, value_rows, grad_rows):
    seq_length = query_rows.shape[0]
    block_rows = min(512, seq_length)
    score_scale = query_rows.shape[1] ** (-0.5)

    def step(carry, block_index):
        grad_key, grad_value = carry
        first_row = block_index * block_rows
        query_block = lax.dynamic_slice_in_dim(query_rows, first_row, block_rows, 0)
        grad_block = lax.dynamic_slice_in_dim(grad_rows, first_row, block_rows, 0)
        scores = jnp.dot(query_block, key_rows.T, preferred_element_type=jnp.float32) * score_scale
        row_max = jnp.max(scores, axis=1, keepdims=True)
        exp_scores = jnp.exp(scores - row_max)
        attn_weights = exp_scores / jnp.sum(exp_scores, axis=1, keepdims=True)
        weights_half = attn_weights.astype(jnp.bfloat16)
        grad_weights = jnp.dot(grad_block, value_rows.T, preferred_element_type=jnp.float32)
        row_dot = jnp.sum(attn_weights * grad_weights, axis=1, keepdims=True)
        grad_scores = (attn_weights * (grad_weights - row_dot)).astype(jnp.bfloat16)
        grad_query = (
            jnp.dot(grad_scores, key_rows, preferred_element_type=jnp.float32) * score_scale
        ).astype(jnp.bfloat16)
        grad_key = grad_key + jnp.dot(
            grad_scores.T, query_block, preferred_element_type=jnp.float32
        )
        grad_value = grad_value + jnp.dot(
            weights_half.T, grad_block, preferred_element_type=jnp.float32
        )
        return ((grad_key, grad_value), grad_query)

    zeros_init = jnp.zeros(query_rows.shape, jnp.float32)
    carry, query_blocks = lax.scan(
        step, (zeros_init, zeros_init), jnp.arange(seq_length // block_rows, dtype=jnp.int32)
    )
    grad_query = query_blocks.reshape(seq_length, -1)
    grad_key = (carry[0] * score_scale).astype(jnp.bfloat16)
    grad_value = carry[1].astype(jnp.bfloat16)
    return (grad_query, grad_key, grad_value)


def heads_backward(query_rows, key_rows, value_rows, grad_rows):
    seq_length = query_rows.shape[0]
    head_count = query_rows.shape[1] // HD

    def split_heads(array):
        return array.reshape(seq_length, head_count, HD).transpose(1, 0, 2)

    def per_head(head_items):
        return attend_back(head_items[0], head_items[1], head_items[2], head_items[3])

    head_grads = lax.map(
        per_head,
        (
            split_heads(query_rows),
            split_heads(key_rows),
            split_heads(value_rows),
            split_heads(grad_rows),
        ),
    )
    return tuple(
        (grads.transpose(1, 0, 2).reshape(seq_length, head_count * HD) for grads in head_grads)
    )


def local(
    rm_hidden, rm_cotangent, rm_gain, rewards, visual_pos, bridge, img_query, img_key, img_value
):
    reward_sum = one_axis_at_a_time(jnp.sum(rewards), DP)
    sample_count = lax.axis_size(DP) * rewards.shape[0]
    reward_weight = rewards[0] * sample_count / reward_sum
    row_offset = lax.axis_index("tensor") * rm_hidden.shape[1]
    local_rows = visual_pos[0] - row_offset
    vis_hidden = jnp.take(rm_hidden[0], local_rows, axis=0)
    vis_cot = jnp.take(rm_cotangent[0], local_rows, axis=0)
    visual_grad = norm_backward(vis_hidden, vis_cot, rm_gain)
    handed = (
        jnp.dot(
            lax.all_gather(visual_grad, "tensor", axis=0, tiled=True),
            bridge,
            preferred_element_type=jnp.float32,
        )
        * reward_weight
    ).astype(jnp.bfloat16)
    grad_rows = upsample(handed)
    head_query, head_key, head_value = (
        lax.all_to_all(img_query[0], "tensor", split_axis=1, concat_axis=0, tiled=True),
        lax.all_to_all(img_key[0], "tensor", split_axis=1, concat_axis=0, tiled=True),
        lax.all_to_all(img_value[0], "tensor", split_axis=1, concat_axis=0, tiled=True),
    )
    head_grads = heads_backward(head_query, head_key, head_value, grad_rows)
    token_query, token_key, token_value = (
        lax.all_to_all(head_grads[0], "tensor", split_axis=0, concat_axis=1, tiled=True),
        lax.all_to_all(head_grads[1], "tensor", split_axis=0, concat_axis=1, tiled=True),
        lax.all_to_all(head_grads[2], "tensor", split_axis=0, concat_axis=1, tiled=True),
    )
    return (token_query[None], token_key[None], token_value[None])


def solution(mesh):
    torus = Mesh(
        mesh.devices.reshape(4, 4, 2, mesh.shape["tensor"]), ("dp_0", "dp_1", "dp_2", "tensor")
    )
    in_specs = (
        P(DP, "tensor", None),
        P(DP, "tensor", None),
        P(),
        P(DP),
        P(DP, "tensor"),
        P(None, "tensor"),
        P(DP, "tensor", None),
        P(DP, "tensor", None),
        P(DP, "tensor", None),
    )
    out_specs = (P(DP, "tensor", None), P(DP, "tensor", None), P(DP, "tensor", None))
    return jax.shard_map(local, mesh=torus, in_specs=in_specs, out_specs=out_specs, check_vma=False)
```

profile of v0, /device:TPU:130, one launch (start us, length us, event | category | flops | bytes accessed | tf_op | source)
XLA Modules:
  0.0 268.8 jit_solution(7245636634787149169)
XLA Ops:
  8.0 2.0 gather_fusion
  10.1 2.0 gather_fusion.1
  12.1 1.1 fusion.18
  13.2 0.9 fusion.23
  15.2 8.6 %all-to-all-start = ((bf16[128,16,128]{2,0,1:T(8,128)(2,1)}), bf16[128,16,128]{2,0,1:T(8,128)(2,1)S(1)}, u32[]{:S(2)}, u32[]{:S(2)}) async-start(bf16[128,16,128]{2,0,1:T(8,128)(2,1)} %copy.21), calls=%async_computation | async-start | bytes 1048576 | tf_op jit(solution)/shard_map/all_to_all | solution.py:118
  24.9 21.7 %all-to-all-done = bf16[128,16,128]{2,0,1:T(8,128)(2,1)S(1)} async-done(((bf16[128,16,128]{2,0,1:T(8,128)(2,1)}), bf16[128,16,128]{2,0,1:T(8,128)(2,1)S(1)}, u32[]{:S(2)}, u32[]{:S(2)}) %all-to-all-start) | async-done | bytes 524320 | tf_op jit(solution)/shard_map/all_to_all | solution.py:118
  46.6 3.6 %all-to-all-start.2 = ((bf16[128,16,128]{2,0,1:T(8,128)(2,1)}), bf16[128,16,128]{2,0,1:T(8,128)(2,1)S(1)}, u32[]{:S(2)}, u32[]{:S(2)}) async-start(bf16[128,16,128]{2,0,1:T(8,128)(2,1)} %copy.23), calls=%async_computation.2 | async-start | bytes 1048576 | tf_op jit(solution)/shard_map/all_to_all | solution.py:120
  51.2 27.4 %all-to-all-done.2 = bf16[128,16,128]{2,0,1:T(8,128)(2,1)S(1)} async-done(((bf16[128,16,128]{2,0,1:T(8,128)(2,1)}), bf16[128,16,128]{2,0,1:T(8,128)(2,1)S(1)}, u32[]{:S(2)}, u32[]{:S(2)}) %all-to-all-start.2) | async-done | bytes 524320 | tf_op jit(solution)/shard_map/all_to_all | solution.py:120
  78.6 3.6 %all-to-all-start.1 = ((bf16[128,16,128]{2,0,1:T(8,128)(2,1)}), bf16[128,16,128]{2,0,1:T(8,128)(2,1)S(1)}, u32[]{:S(2)}, u32[]{:S(2)}) async-start(bf16[128,16,128]{2,0,1:T(8,128)(2,1)} %copy.22), calls=%async_computation.1 | async-start | bytes 1048576 | tf_op jit(solution)/shard_map/all_to_all | solution.py:119
  82.2 9.2 %psum.21 = f32[]{:T(128)} all-reduce(f32[]{:T(128)} %bitcast.7), channel_id=1, replica_groups=mesh['dp_0'=4,'dp_1'=4,'dp_2'=2,'tensor'=16] {'dp_0'}, use_global_device_ids=true, to_apply=%region_2.4 | all-reduce | flops 1 | bytes 8 | tf_op jit(solution)/shard_map/psum | solution.py:14
  91.4 20.0 %psum.22 = f32[]{:T(128)} all-reduce(f32[]{:T(128)} %psum.21), channel_id=1, replica_groups=mesh['dp_0'=4,'dp_1'=4,'dp_2'=2,'tensor'=16] {'dp_1'}, use_global_device_ids=true, to_apply=%region_3.5 | all-reduce | flops 1 | bytes 8 | tf_op jit(solution)/shard_map/psum | solution.py:14
  111.4 3.1 %psum.23 = f32[]{:T(128)} all-reduce(f32[]{:T(128)} %psum.22), channel_id=1, replica_groups=mesh['dp_0'=4,'dp_1'=4,'dp_2'=2,'tensor'=16] {'dp_2'}, use_global_device_ids=true, to_apply=%region_4.0 | all-reduce | flops 1 | bytes 8 | tf_op jit(solution)/shard_map/psum | solution.py:14
  115.9 23.3 %all-gather.2.cloned.1.call-done = bf16[512,3584]{1,0:T(8,128)(2,1)} async-done(((bf16[32,3584]{1,0:T(8,128)(2,1)}), bf16[512,3584]{1,0:T(8,128)(2,1)}) %all-gather.2.cloned.1.call-update) | async-done | bytes 3670032 | tf_op jit(solution)/shard_map/all_gather | solution.py:110
  139.2 3.1 %fusion.17 = bf16[512,128]{1,0:T(8,128)(2,1)S(1)} fusion(bf16[512,3584]{1,0:T(8,128)(2,1)} %all-gather.2.cloned.1.call-done, bf16[3584,128]{1,0:T(8,128)(2,1)S(1)} %copy-done, f32[]{:T(128)S(6)} %div.19), kind=kOutput, calls=%fused_computation.26 | convolution fusion | flops 469893120 | bytes 4718596 | tf_op jit(solution)/shard_map/dot_general | solution.py:109
  142.9 60.4 %while.26 = (s32[]{:T(128)}, f32[2048,128]{1,0:T(8,128)S(1)}, f32[2048,128]{1,0:T(8,128)}, bf16[4,512,128]{2,1,0:T(8,128)(2,1)}, s32[4]{0:T(128)S(1)}, /*index=5...) while((s32[]{:T(128)}, f32[2048,128]{1,0:T(8,128)S(1)}, ...), condition=%wide.region_9.11_spmd.clone, body=%wide.region_5.10_spmd.clone.sunk | while | flops 1364326912 | bytes 77749032 | solution.py:64
  144.9 1.9 copy-done.1
  147.7 4.5 %convolution_add_fusion.5 = f32[2048,128]{1,0:T(8,128)} fusion(f32[2048,128]{1,0:T(8,128)} %get-tuple-element.219, pred[]{:T(512)S(6)} %compare.3, bf16[2048,128]{1,0:T(8,128)(2,1)S(1)} %get-tuple-element.237, s32[]{:T(128)S(6)} %select_n.33, f32[512,2048]{1,0:T(8,128)} %copy-done.1, f32[512]{0:T(512)S(1)} %fusion.50, f32[512]{0:T(512)S(1)} %get-tuple-element.201), kind=kOutput, calls=%fused_computation.8.clone.1 | convolution fusion | flops 273154048 | bytes 6426629 | tf_op jit(solution)/shard_map/while/body/eval_jaxpr/while/body/eval_jaxpr/dot_general | solution.py:58
  152.2 1.5 multiply_reduce_fusion.5
  153.8 1.4 multiply_convert_fusion.3
  155.2 1.2 convolution_add_fusion.4
  156.4 1.4 fusion.51
  159.8 1.9 copy-done.1
  162.6 4.8 %convolution_add_fusion.5 = f32[2048,128]{1,0:T(8,128)} fusion(f32[2048,128]{1,0:T(8,128)} %get-tuple-element.219, pred[]{:T(512)S(6)} %compare.3, bf16[2048,128]{1,0:T(8,128)(2,1)S(1)} %get-tuple-element.237, s32[]{:T(128)S(6)} %select_n.33, f32[512,2048]{1,0:T(8,128)} %copy-done.1, f32[512]{0:T(512)S(1)} %fusion.50, f32[512]{0:T(512)S(1)} %get-tuple-element.201), kind=kOutput, calls=%fused_computation.8.clone.1 | convolution fusion | flops 273154048 | bytes 6426629 | tf_op jit(solution)/shard_map/while/body/eval_jaxpr/while/body/eval_jaxpr/dot_general | solution.py:58
  167.4 1.5 multiply_reduce_fusion.5
  168.9 1.4 multiply_convert_fusion.3
  170.4 1.2 convolution_add_fusion.4
  171.6 1.4 fusion.51
  175.0 1.9 copy-done.1
  177.7 4.8 %convolution_add_fusion.5 = f32[2048,128]{1,0:T(8,128)} fusion(f32[2048,128]{1,0:T(8,128)} %get-tuple-element.219, pred[]{:T(512)S(6)} %compare.3, bf16[2048,128]{1,0:T(8,128)(2,1)S(1)} %get-tuple-element.237, s32[]{:T(128)S(6)} %select_n.33, f32[512,2048]{1,0:T(8,128)} %copy-done.1, f32[512]{0:T(512)S(1)} %fusion.50, f32[512]{0:T(512)S(1)} %get-tuple-element.201), kind=kOutput, calls=%fused_computation.8.clone.1 | convolution fusion | flops 273154048 | bytes 6426629 | tf_op jit(solution)/shard_map/while/body/eval_jaxpr/while/body/eval_jaxpr/dot_general | solution.py:58
  182.6 1.5 multiply_reduce_fusion.5
  184.1 1.4 multiply_convert_fusion.3
  185.5 1.2 convolution_add_fusion.4
  186.7 1.4 fusion.51
  190.1 1.9 copy-done.1
  192.9 4.8 %convolution_add_fusion.5 = f32[2048,128]{1,0:T(8,128)} fusion(f32[2048,128]{1,0:T(8,128)} %get-tuple-element.219, pred[]{:T(512)S(6)} %compare.3, bf16[2048,128]{1,0:T(8,128)(2,1)S(1)} %get-tuple-element.237, s32[]{:T(128)S(6)} %select_n.33, f32[512,2048]{1,0:T(8,128)} %copy-done.1, f32[512]{0:T(512)S(1)} %fusion.50, f32[512]{0:T(512)S(1)} %get-tuple-element.201), kind=kOutput, calls=%fused_computation.8.clone.1 | convolution fusion | flops 273154048 | bytes 6426629 | tf_op jit(solution)/shard_map/while/body/eval_jaxpr/while/body/eval_jaxpr/dot_general | solution.py:58
  197.8 1.5 multiply_reduce_fusion.5
  199.3 1.4 multiply_convert_fusion.3
  200.7 1.2 convolution_add_fusion.4
  201.9 1.4 fusion.51
  204.2 5.5 %all-to-all-start.4 = ((bf16[16,128,128]{2,1,0:T(8,128)(2,1)}), bf16[16,128,128]{2,1,0:T(8,128)(2,1)S(1)}, u32[]{:S(2)}, u32[]{:S(2)}) async-start(bf16[16,128,128]{2,1,0:T(8,128)(2,1)} %bitcast.16), calls=%async_computation.4 | async-start | bytes 1048576 | tf_op jit(solution)/shard_map/all_to_all | solution.py:125
  209.6 1.3 convert_element_type.34
  210.9 12.4 %all-to-all-done.4 = bf16[16,128,128]{2,1,0:T(8,128)(2,1)S(1)} async-done(((bf16[16,128,128]{2,1,0:T(8,128)(2,1)}), bf16[16,128,128]{2,1,0:T(8,128)(2,1)S(1)}, u32[]{:S(2)}, u32[]{:S(2)}) %all-to-all-start.4) | async-done | bytes 524320 | tf_op jit(solution)/shard_map/all_to_all | solution.py:125
  223.4 18.3 %all_to_all.96 = bf16[16,128,128]{2,1,0:T(8,128)(2,1)S(1)} all-to-all(bf16[16,128,128]{2,1,0:T(8,128)(2,1)S(1)} %bitcast.70), channel_id=1, replica_groups=mesh['dp_0'=4,'dp_1'=4,'dp_2'=2,'tensor'=16] {'tensor'}, dimensions={0} | all-to-all | bytes 1048576 | tf_op jit(solution)/shard_map/all_to_all | solution.py:126
  241.7 3.6 %all-to-all-start.3 = ((bf16[16,128,128]{2,1,0:T(8,128)(2,1)}), bf16[16,128,128]{2,1,0:T(8,128)(2,1)S(1)}, u32[]{:S(2)}, u32[]{:S(2)}) async-start(bf16[16,128,128]{2,1,0:T(8,128)(2,1)} %bitcast.13), calls=%async_computation.3 | async-start | bytes 1048576 | tf_op jit(solution)/shard_map/all_to_all | solution.py:124
  245.5 1.0 copy.28
  246.8 1.0 copy.29
  247.8 12.9 %all-to-all-done.3 = bf16[16,128,128]{2,1,0:T(8,128)(2,1)S(1)} async-done(((bf16[16,128,128]{2,1,0:T(8,128)(2,1)}), bf16[16,128,128]{2,1,0:T(8,128)(2,1)S(1)}, u32[]{:S(2)}, u32[]{:S(2)}) %all-to-all-start.3) | async-done | bytes 524320 | tf_op jit(solution)/shard_map/all_to_all | solution.py:124
  261.0 1.0 copy.27
  (66 shorter events, 15.0 us)
Async XLA Ops:
  7.2 132.0 %copy-start = (bf16[3584,128]{1,0:T(8,128)(2,1)S(1)}, bf16[3584,128]{1,0:T(8,128)(2,1)}, u32[]{:S(2)}) copy-start(bf16[3584,128]{1,0:T(8,128)(2,1)} %param.18) | copy-start | bytes 2752516
  7.2 6.0 %copy-start.8 = (f32[3584]{0:T(1024)S(1)}, f32[3584]{0:T(1024)}, u32[]{:S(2)}) copy-start(f32[3584]{0:T(1024)} %param.15) | copy-start | bytes 43012
  7.2 7.0 %copy-start.3 = (bf16[1,128,2048]{2,1,0:T(8,128)(2,1)S(1)}, bf16[1,128,2048]{2,1,0:T(8,128)(2,1)}, u32[]{:S(2)}) copy-start(bf16[1,128,2048]{2,1,0:T(8,128)(2,1)} %param.19) | copy-start | bytes 1572868
  7.2 132.0 %all-gather.2.cloned.1.call-start = ((), (), s32[]{:S(2)}) async-start(), calls=%async_computation.6 | async-start | bytes 3899392 | tf_op jit(solution)/shard_map/all_gather | solution.py:110
  8.0 15.8 %copy-start.4 = (bf16[1,128,2048]{2,1,0:T(8,128)(2,1)S(1)}, bf16[1,128,2048]{2,1,0:T(8,128)(2,1)}, u32[]{:S(2)}) copy-start(bf16[1,128,2048]{2,1,0:T(8,128)(2,1)} %param.21) | copy-start | bytes 1572868
  12.1 38.1 %copy-start.5 = (bf16[1,128,2048]{2,1,0:T(8,128)(2,1)S(1)}, bf16[1,128,2048]{2,1,0:T(8,128)(2,1)}, u32[]{:S(2)}) copy-start(bf16[1,128,2048]{2,1,0:T(8,128)(2,1)} %param.20) | copy-start | bytes 1572868
  15.2 31.4 %all-to-all-start = ((bf16[128,16,128]{2,0,1:T(8,128)(2,1)}), bf16[128,16,128]{2,0,1:T(8,128)(2,1)S(1)}, u32[]{:S(2)}, u32[]{:S(2)}) async-start(bf16[128,16,128]{2,0,1:T(8,128)(2,1)} %copy.21), calls=%async_computation | async-start | bytes 1048576 | tf_op jit(solution)/shard_map/all_to_all | solution.py:118
  46.6 32.0 %all-to-all-start.2 = ((bf16[128,16,128]{2,0,1:T(8,128)(2,1)}), bf16[128,16,128]{2,0,1:T(8,128)(2,1)S(1)}, u32[]{:S(2)}, u32[]{:S(2)}) async-start(bf16[128,16,128]{2,0,1:T(8,128)(2,1)} %copy.23), calls=%async_computation.2 | async-start | bytes 1048576 | tf_op jit(solution)/shard_map/all_to_all | solution.py:120
  78.6 36.0 %copy-start.6 = (bf16[128,16,128]{2,0,1:T(8,128)(2,1)}, bf16[128,16,128]{2,0,1:T(8,128)(2,1)S(1)}, u32[]{:S(2)}) copy-start(bf16[128,16,128]{2,0,1:T(8,128)(2,1)S(1)} %all-to-all-done.2) | copy-start | bytes 1572868
  78.6 63.7 %all-to-all-start.1 = ((bf16[128,16,128]{2,0,1:T(8,128)(2,1)}), bf16[128,16,128]{2,0,1:T(8,128)(2,1)S(1)}, u32[]{:S(2)}, u32[]{:S(2)}) async-start(bf16[128,16,128]{2,0,1:T(8,128)(2,1)} %copy.22), calls=%async_computation.1 | async-start | bytes 1048576 | tf_op jit(solution)/shard_map/all_to_all | solution.py:119
  144.9 1.9 copy-start.1
  147.7 4.6 %copy-start.2 = (f32[512,2048]{1,0:T(8,128)S(1)}, f32[512,2048]{1,0:T(8,128)}, u32[]{:S(2)}) copy-start(f32[512,2048]{1,0:T(8,128)} %copy-done.1) | copy-start | bytes 12582916 | tf_op jit(solution)/shard_map/while/body/eval_jaxpr/while
  147.7 4.6 %copy-start.7 = (bf16[2048,128]{1,0:T(8,128)(2,1)S(1)}, bf16[2048,128]{1,0:T(8,128)(2,1)}, u32[]{:S(2)}) copy-start(bf16[2048,128]{1,0:T(8,128)(2,1)} %get-tuple-element.238) | copy-start | bytes 1572868 | tf_op jit(solution)/shard_map/while/body/eval_jaxpr/while
  159.8 1.9 copy-start.1
  162.5 4.9 %copy-start.2 = (f32[512,2048]{1,0:T(8,128)S(1)}, f32[512,2048]{1,0:T(8,128)}, u32[]{:S(2)}) copy-start(f32[512,2048]{1,0:T(8,128)} %copy-done.1) | copy-start | bytes 12582916 | tf_op jit(solution)/shard_map/while/body/eval_jaxpr/while
  162.6 4.8 %copy-start.7 = (bf16[2048,128]{1,0:T(8,128)(2,1)S(1)}, bf16[2048,128]{1,0:T(8,128)(2,1)}, u32[]{:S(2)}) copy-start(bf16[2048,128]{1,0:T(8,128)(2,1)} %get-tuple-element.238) | copy-start | bytes 1572868 | tf_op jit(solution)/shard_map/while/body/eval_jaxpr/while
  175.0 1.9 copy-start.1
  177.7 4.9 %copy-start.2 = (f32[512,2048]{1,0:T(8,128)S(1)}, f32[512,2048]{1,0:T(8,128)}, u32[]{:S(2)}) copy-start(f32[512,2048]{1,0:T(8,128)} %copy-done.1) | copy-start | bytes 12582916 | tf_op jit(solution)/shard_map/while/body/eval_jaxpr/while
  177.7 4.8 %copy-start.7 = (bf16[2048,128]{1,0:T(8,128)(2,1)S(1)}, bf16[2048,128]{1,0:T(8,128)(2,1)}, u32[]{:S(2)}) copy-start(bf16[2048,128]{1,0:T(8,128)(2,1)} %get-tuple-element.238) | copy-start | bytes 1572868 | tf_op jit(solution)/shard_map/while/body/eval_jaxpr/while
  190.1 1.9 copy-start.1
  192.9 4.9 %copy-start.2 = (f32[512,2048]{1,0:T(8,128)S(1)}, f32[512,2048]{1,0:T(8,128)}, u32[]{:S(2)}) copy-start(f32[512,2048]{1,0:T(8,128)} %copy-done.1) | copy-start | bytes 12582916 | tf_op jit(solution)/shard_map/while/body/eval_jaxpr/while
  192.9 4.8 %copy-start.7 = (bf16[2048,128]{1,0:T(8,128)(2,1)S(1)}, bf16[2048,128]{1,0:T(8,128)(2,1)}, u32[]{:S(2)}) copy-start(bf16[2048,128]{1,0:T(8,128)(2,1)} %get-tuple-element.238) | copy-start | bytes 1572868 | tf_op jit(solution)/shard_map/while/body/eval_jaxpr/while
  204.2 19.2 %all-to-all-start.4 = ((bf16[16,128,128]{2,1,0:T(8,128)(2,1)}), bf16[16,128,128]{2,1,0:T(8,128)(2,1)S(1)}, u32[]{:S(2)}, u32[]{:S(2)}) async-start(bf16[16,128,128]{2,1,0:T(8,128)(2,1)} %bitcast.16), calls=%async_computation.4 | async-start | bytes 1048576 | tf_op jit(solution)/shard_map/all_to_all | solution.py:125
  241.7 19.0 %all-to-all-start.3 = ((bf16[16,128,128]{2,1,0:T(8,128)(2,1)}), bf16[16,128,128]{2,1,0:T(8,128)(2,1)S(1)}, u32[]{:S(2)}, u32[]{:S(2)}) async-start(bf16[16,128,128]{2,1,0:T(8,128)(2,1)} %bitcast.13), calls=%async_computation.3 | async-start | bytes 1048576 | tf_op jit(solution)/shard_map/all_to_all | solution.py:124
Sparse Core Ops, SparseCore 0:
  14.3 124.8 all-gather.1
where the time goes:
time: 270 us; the launch traced here: 269 us
  waiting for transfers between devices  97.6 us (36%)
  blocking collectives  50.7 us (19%)
  matrix products  41.8 us (15%)
  starting transfers between devices  24.9 us (9%)
  local copies, waits for them, and re-layouts  21.7 us (8%)
  between operations  15.6 us (6%)
  other arithmetic  13.8 us (5%)
  loops' own time  2.84 us (1%)
    psum x3, blocking collectives, one_axis_at_a_time(): return functools.reduce(lax.psum, axes, array)  32.4 us
    all_to_all x1, waiting for transfers between devices, local(): lax.all_to_all(img_value[0], 'tensor', split_axis=1, concat_axis=0, tiled...  27.4 us
    all_gather x1, waiting for transfers between devices, local(): lax.all_gather(visual_grad, 'tensor', axis=0, tiled=True)  23.3 us
    all_to_all x1, waiting for transfers between devices, local(): lax.all_to_all(img_query[0], 'tensor', split_axis=1, concat_axis=0, tiled...  21.7 us
    dot_general x4, matrix products, step(): jnp.dot(weights_half.T, grad_block, preferred_element_type=jnp.float32)  19 us
    all_to_all x1, blocking collectives, local(): lax.all_to_all(head_grads[2], 'tensor', split_axis=0, concat_axis=1, tile...  18.3 us
    all_to_all x1, waiting for transfers between devices, local(): lax.all_to_all(head_grads[0], 'tensor', split_axis=0, concat_axis=1, tile...  12.9 us
    all_to_all x1, waiting for transfers between devices, local(): lax.all_to_all(head_grads[1], 'tensor', split_axis=0, concat_axis=1, tile...  12.4 us
  transfers between devices with their start and end apart: 6, of which 5 were waited for; matrix products, arithmetic and copies ran while one was open for 4% of the time, Pallas kernels for 0%

commit v1 on v0

--- a/solution.py
+++ b/solution.py
@@ -107,7 +107,10 @@
     visual_grad = norm_backward(vis_hidden, vis_cot, rm_gain)
     handed = (
         jnp.dot(
-            lax.all_gather(visual_grad, "tensor", axis=0, tiled=True),
+            jnp.concatenate(
+                lax.all_to_all(jnp.stack([visual_grad] * lax.axis_size("tensor")), "tensor", 0, 0),
+                axis=0,
+            ),
             bridge,
             preferred_element_type=jnp.float32,
         )

time: 270 us -> 307 us (1.14)
  the two profiles are of different devices: /device:TPU:130 before, /device:TPU:1 now
where the time goes in v1:
time: 307 us; the launch traced here: 306 us
  waiting for transfers between devices  137 us (45%)
  blocking collectives  53.5 us (17%)
  matrix products  41.8 us (14%)
  starting transfers between devices  33.2 us (11%)
  local copies, waits for them, and re-layouts  23.4 us (8%)
  other arithmetic  11.6 us (4%)
    all_to_all x1, waiting for transfers between devices, local(): lax.all_to_all(jnp.stack([visual_grad] * lax.axis_size('tensor')), 'tenso...  82.4 us
    psum x3, blocking collectives, one_axis_at_a_time(): return functools.reduce(lax.psum, axes, array)  33.9 us
    all_to_all x1, blocking collectives, local(): lax.all_to_all(head_grads[2], 'tensor', split_axis=0, concat_axis=1, tile...  19.6 us
    dot_general x4, matrix products, step(): jnp.dot(weights_half.T, grad_block, preferred_element_type=jnp.float32)  19 us
    all_to_all x1, waiting for transfers between devices, local(): lax.all_to_all(head_grads[1], 'tensor', split_axis=0, concat_axis=1, tile...  14.5 us
    all_to_all x1, waiting for transfers between devices, local(): lax.all_to_all(img_query[0], 'tensor', split_axis=1, concat_axis=0, tiled...  13.6 us
    all_to_all x1, waiting for transfers between devices, local(): lax.all_to_all(img_value[0], 'tensor', split_axis=1, concat_axis=0, tiled...  13.6 us
    all_to_all x1, waiting for transfers between devices, local(): lax.all_to_all(head_grads[0], 'tensor', split_axis=0, concat_axis=1, tile...  13.1 us
  transfers between devices with their start and end apart: 6, of which 5 were waited for; matrix products, arithmetic and copies ran while one was open for 4% of the time, Pallas kernels for 0%

profile of v1, /device:TPU:1, one launch (start us, length us, event | category | flops | bytes accessed | tf_op | source)
XLA Modules:
  0.0 305.9 jit_solution(9474468032274344607)
XLA Ops:
  0.7 1.3 copy.30
  2.9 9.3 %all-to-all-start = ((bf16[128,16,128]{2,0,1:T(8,128)(2,1)}), bf16[128,16,128]{2,0,1:T(8,128)(2,1)S(1)}, u32[]{:S(2)}, u32[]{:S(2)}) async-start(bf16[128,16,128]{2,0,1:T(8,128)(2,1)} %copy.21), calls=%async_computation | async-start | bytes 1048576 | tf_op jit(solution)/shard_map/all_to_all | solution.py:121
  12.2 1.1 copy.32
  14.3 13.6 %all-to-all-done = bf16[128,16,128]{2,0,1:T(8,128)(2,1)S(1)} async-done(((bf16[128,16,128]{2,0,1:T(8,128)(2,1)}), bf16[128,16,128]{2,0,1:T(8,128)(2,1)S(1)}, u32[]{:S(2)}, u32[]{:S(2)}) %all-to-all-start) | async-done | bytes 524320 | tf_op jit(solution)/shard_map/all_to_all | solution.py:121
  27.9 3.6 %all-to-all-start.3 = ((bf16[128,16,128]{2,0,1:T(8,128)(2,1)}), bf16[128,16,128]{2,0,1:T(8,128)(2,1)S(1)}, u32[]{:S(2)}, u32[]{:S(2)}) async-start(bf16[128,16,128]{2,0,1:T(8,128)(2,1)} %copy.23), calls=%async_computation.3 | async-start | bytes 1048576 | tf_op jit(solution)/shard_map/all_to_all | solution.py:123
  33.5 13.6 %all-to-all-done.3 = bf16[128,16,128]{2,0,1:T(8,128)(2,1)S(1)} async-done(((bf16[128,16,128]{2,0,1:T(8,128)(2,1)}), bf16[128,16,128]{2,0,1:T(8,128)(2,1)S(1)}, u32[]{:S(2)}, u32[]{:S(2)}) %all-to-all-start.3) | async-done | bytes 524320 | tf_op jit(solution)/shard_map/all_to_all | solution.py:123
  47.2 2.2 stack.2
  49.4 4.6 %all-to-all-start.2 = ((bf16[16,32,3584]{2,1,0:T(8,128)(2,1)}), bf16[16,32,3584]{2,1,0:T(8,128)(2,1)}, u32[]{:S(2)}, u32[]{:S(2)}) async-start(bf16[16,32,3584]{2,1,0:T(8,128)(2,1)} %stack.2), calls=%async_computation.2 | async-start | bytes 7340032 | tf_op jit(solution)/shard_map/all_to_all | solution.py:111
  55.1 82.4 %all-to-all-done.2 = bf16[16,32,3584]{2,1,0:T(8,128)(2,1)} async-done(((bf16[16,32,3584]{2,1,0:T(8,128)(2,1)}), bf16[16,32,3584]{2,1,0:T(8,128)(2,1)}, u32[]{:S(2)}, u32[]{:S(2)}) %all-to-all-start.2) | async-done | bytes 3670048 | tf_op jit(solution)/shard_map/all_to_all | solution.py:111
  137.5 4.4 %all-to-all-start.1 = ((bf16[128,16,128]{2,0,1:T(8,128)(2,1)}), bf16[128,16,128]{2,0,1:T(8,128)(2,1)S(1)}, u32[]{:S(2)}, u32[]{:S(2)}) async-start(bf16[128,16,128]{2,0,1:T(8,128)(2,1)} %copy.22), calls=%async_computation.1 | async-start | bytes 1048576 | tf_op jit(solution)/shard_map/all_to_all | solution.py:122
  141.8 9.7 %psum.21 = f32[]{:T(128)} all-reduce(f32[]{:T(128)} %bitcast.8), channel_id=1, replica_groups=mesh['dp_0'=4,'dp_1'=4,'dp_2'=2,'tensor'=16] {'dp_0'}, use_global_device_ids=true, to_apply=%region_2.4 | all-reduce | flops 1 | bytes 8 | tf_op jit(solution)/shard_map/psum | solution.py:14
  151.6 17.1 %psum.22 = f32[]{:T(128)} all-reduce(f32[]{:T(128)} %psum.21), channel_id=1, replica_groups=mesh['dp_0'=4,'dp_1'=4,'dp_2'=2,'tensor'=16] {'dp_1'}, use_global_device_ids=true, to_apply=%region_3.5 | all-reduce | flops 1 | bytes 8 | tf_op jit(solution)/shard_map/psum | solution.py:14
  168.7 7.0 %psum.23 = f32[]{:T(128)} all-reduce(f32[]{:T(128)} %psum.22), channel_id=1, replica_groups=mesh['dp_0'=4,'dp_1'=4,'dp_2'=2,'tensor'=16] {'dp_2'}, use_global_device_ids=true, to_apply=%region_4.0 | all-reduce | flops 1 | bytes 8 | tf_op jit(solution)/shard_map/psum | solution.py:14
  177.2 3.1 %fusion.17 = bf16[512,128]{1,0:T(8,128)(2,1)S(1)} fusion(bf16[512,3584]{1,0:T(8,128)(2,1)} %bitcast.7, bf16[3584,128]{1,0:T(8,128)(2,1)S(1)} %copy-done, f32[]{:T(128)S(6)} %div.19), kind=kOutput, calls=%fused_computation.26 | convolution fusion | flops 469893120 | bytes 4718596 | tf_op jit(solution)/shard_map/dot_general | solution.py:109
  180.9 60.4 %while.26 = (s32[]{:T(128)}, f32[2048,128]{1,0:T(8,128)S(1)}, f32[2048,128]{1,0:T(8,128)}, bf16[4,512,128]{2,1,0:T(8,128)(2,1)}, s32[4]{0:T(128)S(1)}, /*index=5...) while((s32[]{:T(128)}, f32[2048,128]{1,0:T(8,128)S(1)}, ...), condition=%wide.region_9.11_spmd.clone, body=%wide.region_5.10_spmd.clone.sunk | while | flops 1364326912 | bytes 77749032 | solution.py:64
  182.9 1.9 copy-done.1
  185.7 4.5 %convolution_add_fusion.5 = f32[2048,128]{1,0:T(8,128)} fusion(f32[2048,128]{1,0:T(8,128)} %get-tuple-element.219, pred[]{:T(512)S(6)} %compare.3, bf16[2048,128]{1,0:T(8,128)(2,1)S(1)} %get-tuple-element.237, s32[]{:T(128)S(6)} %select_n.33, f32[512,2048]{1,0:T(8,128)} %copy-done.1, f32[512]{0:T(512)S(1)} %fusion.50, f32[512]{0:T(512)S(1)} %get-tuple-element.201), kind=kOutput, calls=%fused_computation.8.clone.1 | convolution fusion | flops 273154048 | bytes 6426629 | tf_op jit(solution)/shard_map/while/body/eval_jaxpr/while/body/eval_jaxpr/dot_general | solution.py:58
  190.2 1.5 multiply_reduce_fusion.5
  191.8 1.4 multiply_convert_fusion.3
  193.2 1.2 convolution_add_fusion.4
  194.4 1.4 fusion.51
  197.8 1.9 copy-done.1
  200.6 4.8 %convolution_add_fusion.5 = f32[2048,128]{1,0:T(8,128)} fusion(f32[2048,128]{1,0:T(8,128)} %get-tuple-element.219, pred[]{:T(512)S(6)} %compare.3, bf16[2048,128]{1,0:T(8,128)(2,1)S(1)} %get-tuple-element.237, s32[]{:T(128)S(6)} %select_n.33, f32[512,2048]{1,0:T(8,128)} %copy-done.1, f32[512]{0:T(512)S(1)} %fusion.50, f32[512]{0:T(512)S(1)} %get-tuple-element.201), kind=kOutput, calls=%fused_computation.8.clone.1 | convolution fusion | flops 273154048 | bytes 6426629 | tf_op jit(solution)/shard_map/while/body/eval_jaxpr/while/body/eval_jaxpr/dot_general | solution.py:58
  205.4 1.5 multiply_reduce_fusion.5
  206.9 1.4 multiply_convert_fusion.3
  208.4 1.2 convolution_add_fusion.4
  209.5 1.4 fusion.51
  213.0 1.9 copy-done.1
  215.7 4.8 %convolution_add_fusion.5 = f32[2048,128]{1,0:T(8,128)} fusion(f32[2048,128]{1,0:T(8,128)} %get-tuple-element.219, pred[]{:T(512)S(6)} %compare.3, bf16[2048,128]{1,0:T(8,128)(2,1)S(1)} %get-tuple-element.237, s32[]{:T(128)S(6)} %select_n.33, f32[512,2048]{1,0:T(8,128)} %copy-done.1, f32[512]{0:T(512)S(1)} %fusion.50, f32[512]{0:T(512)S(1)} %get-tuple-element.201), kind=kOutput, calls=%fused_computation.8.clone.1 | convolution fusion | flops 273154048 | bytes 6426629 | tf_op jit(solution)/shard_map/while/body/eval_jaxpr/while/body/eval_jaxpr/dot_general | solution.py:58
  220.6 1.5 multiply_reduce_fusion.5
  222.1 1.4 multiply_convert_fusion.3
  223.5 1.2 convolution_add_fusion.4
  224.7 1.4 fusion.51
  228.1 1.9 copy-done.1
  230.9 4.8 %convolution_add_fusion.5 = f32[2048,128]{1,0:T(8,128)} fusion(f32[2048,128]{1,0:T(8,128)} %get-tuple-element.219, pred[]{:T(512)S(6)} %compare.3, bf16[2048,128]{1,0:T(8,128)(2,1)S(1)} %get-tuple-element.237, s32[]{:T(128)S(6)} %select_n.33, f32[512,2048]{1,0:T(8,128)} %copy-done.1, f32[512]{0:T(512)S(1)} %fusion.50, f32[512]{0:T(512)S(1)} %get-tuple-element.201), kind=kOutput, calls=%fused_computation.8.clone.1 | convolution fusion | flops 273154048 | bytes 6426629 | tf_op jit(solution)/shard_map/while/body/eval_jaxpr/while/body/eval_jaxpr/dot_general | solution.py:58
  235.8 1.5 multiply_reduce_fusion.5
  237.3 1.4 multiply_convert_fusion.3
  238.7 1.2 convolution_add_fusion.4
  239.9 1.4 fusion.51
  242.2 7.4 %all-to-all-start.5 = ((bf16[16,128,128]{2,1,0:T(8,128)(2,1)}), bf16[16,128,128]{2,1,0:T(8,128)(2,1)S(1)}, u32[]{:S(2)}, u32[]{:S(2)}) async-start(bf16[16,128,128]{2,1,0:T(8,128)(2,1)} %bitcast.17), calls=%async_computation.5 | async-start | bytes 1048576 | tf_op jit(solution)/shard_map/all_to_all | solution.py:128
  249.5 1.3 convert_element_type.34
  250.8 14.5 %all-to-all-done.5 = bf16[16,128,128]{2,1,0:T(8,128)(2,1)S(1)} async-done(((bf16[16,128,128]{2,1,0:T(8,128)(2,1)}), bf16[16,128,128]{2,1,0:T(8,128)(2,1)S(1)}, u32[]{:S(2)}, u32[]{:S(2)}) %all-to-all-start.5) | async-done | bytes 524320 | tf_op jit(solution)/shard_map/all_to_all | solution.py:128
  265.3 19.6 %all_to_all.101 = bf16[16,128,128]{2,1,0:T(8,128)(2,1)S(1)} all-to-all(bf16[16,128,128]{2,1,0:T(8,128)(2,1)S(1)} %bitcast.71), channel_id=1, replica_groups=mesh['dp_0'=4,'dp_1'=4,'dp_2'=2,'tensor'=16] {'tensor'}, dimensions={0} | all-to-all | bytes 1048576 | tf_op jit(solution)/shard_map/all_to_all | solution.py:129
  284.9 4.0 %all-to-all-start.4 = ((bf16[16,128,128]{2,1,0:T(8,128)(2,1)}), bf16[16,128,128]{2,1,0:T(8,128)(2,1)S(1)}, u32[]{:S(2)}, u32[]{:S(2)}) async-start(bf16[16,128,128]{2,1,0:T(8,128)(2,1)} %bitcast.14), calls=%async_computation.4 | async-start | bytes 1048576 | tf_op jit(solution)/shard_map/all_to_all | solution.py:127
  289.2 1.0 copy.28
  290.5 1.0 copy.29
  291.5 13.1 %all-to-all-done.4 = bf16[16,128,128]{2,1,0:T(8,128)(2,1)S(1)} async-done(((bf16[16,128,128]{2,1,0:T(8,128)(2,1)}), bf16[16,128,128]{2,1,0:T(8,128)(2,1)S(1)}, u32[]{:S(2)}, u32[]{:S(2)}) %all-to-all-start.4) | async-done | bytes 524320 | tf_op jit(solution)/shard_map/all_to_all | solution.py:127
  304.9 1.0 copy.27
  (68 shorter events, 15.9 us)
Async XLA Ops:
  0.6 176.5 %copy-start = (bf16[3584,128]{1,0:T(8,128)(2,1)S(1)}, bf16[3584,128]{1,0:T(8,128)(2,1)}, u32[]{:S(2)}) copy-start(bf16[3584,128]{1,0:T(8,128)(2,1)} %param.18) | copy-start | bytes 2752516
  0.6 30.9 %copy-start.9 = (s32[1,32]{1,0:T(1,128)S(1)}, s32[1,32]{1,0:T(1,128)}, u32[]{:S(2)}) copy-start(s32[1,32]{1,0:T(1,128)} %param.17) | copy-start | bytes 388
  0.7 30.9 %copy-start.3 = (bf16[1,64,3584]{2,1,0:T(8,128)(2,1)S(1)}, bf16[1,64,3584]{2,1,0:T(8,128)(2,1)}, u32[]{:S(2)}) copy-start(bf16[1,64,3584]{2,1,0:T(8,128)(2,1)} %param.13) | copy-start | bytes 1376260
  0.7 31.6 %copy-start.4 = (bf16[1,64,3584]{2,1,0:T(8,128)(2,1)S(1)}, bf16[1,64,3584]{2,1,0:T(8,128)(2,1)}, u32[]{:S(2)}) copy-start(bf16[1,64,3584]{2,1,0:T(8,128)(2,1)} %param.14) | copy-start | bytes 1376260
  2.9 30.1 %copy-start.8 = (f32[3584]{0:T(1024)S(1)}, f32[3584]{0:T(1024)}, u32[]{:S(2)}) copy-start(f32[3584]{0:T(1024)} %param.15) | copy-start | bytes 43012
  2.9 25.0 %all-to-all-start = ((bf16[128,16,128]{2,0,1:T(8,128)(2,1)}), bf16[128,16,128]{2,0,1:T(8,128)(2,1)S(1)}, u32[]{:S(2)}, u32[]{:S(2)}) async-start(bf16[128,16,128]{2,0,1:T(8,128)(2,1)} %copy.21), calls=%async_computation | async-start | bytes 1048576 | tf_op jit(solution)/shard_map/all_to_all | solution.py:121
  27.9 19.2 %all-to-all-start.3 = ((bf16[128,16,128]{2,0,1:T(8,128)(2,1)}), bf16[128,16,128]{2,0,1:T(8,128)(2,1)S(1)}, u32[]{:S(2)}, u32[]{:S(2)}) async-start(bf16[128,16,128]{2,0,1:T(8,128)(2,1)} %copy.23), calls=%async_computation.3 | async-start | bytes 1048576 | tf_op jit(solution)/shard_map/all_to_all | solution.py:123
  47.2 2.2 copy-start.6
  49.4 4.6 %copy-start.5 = (bf16[1,128,2048]{2,1,0:T(8,128)(2,1)S(1)}, bf16[1,128,2048]{2,1,0:T(8,128)(2,1)}, u32[]{:S(2)}) copy-start(bf16[1,128,2048]{2,1,0:T(8,128)(2,1)} %param.20) | copy-start | bytes 1572868
  49.4 88.1 %all-to-all-start.2 = ((bf16[16,32,3584]{2,1,0:T(8,128)(2,1)}), bf16[16,32,3584]{2,1,0:T(8,128)(2,1)}, u32[]{:S(2)}, u32[]{:S(2)}) async-start(bf16[16,32,3584]{2,1,0:T(8,128)(2,1)} %stack.2), calls=%async_computation.2 | async-start | bytes 7340032 | tf_op jit(solution)/shard_map/all_to_all | solution.py:111
  137.5 42.8 %all-to-all-start.1 = ((bf16[128,16,128]{2,0,1:T(8,128)(2,1)}), bf16[128,16,128]{2,0,1:T(8,128)(2,1)S(1)}, u32[]{:S(2)}, u32[]{:S(2)}) async-start(bf16[128,16,128]{2,0,1:T(8,128)(2,1)} %copy.22), calls=%async_computation.1 | async-start | bytes 1048576 | tf_op jit(solution)/shard_map/all_to_all | solution.py:122
  182.9 1.9 copy-start.1
  185.7 4.6 %copy-start.2 = (f32[512,2048]{1,0:T(8,128)S(1)}, f32[512,2048]{1,0:T(8,128)}, u32[]{:S(2)}) copy-start(f32[512,2048]{1,0:T(8,128)} %copy-done.1) | copy-start | bytes 12582916 | tf_op jit(solution)/shard_map/while/body/eval_jaxpr/while
  185.7 4.6 %copy-start.7 = (bf16[2048,128]{1,0:T(8,128)(2,1)S(1)}, bf16[2048,128]{1,0:T(8,128)(2,1)}, u32[]{:S(2)}) copy-start(bf16[2048,128]{1,0:T(8,128)(2,1)} %get-tuple-element.238) | copy-start | bytes 1572868 | tf_op jit(solution)/shard_map/while/body/eval_jaxpr/while
  197.8 1.9 copy-start.1
  200.5 4.9 %copy-start.2 = (f32[512,2048]{1,0:T(8,128)S(1)}, f32[512,2048]{1,0:T(8,128)}, u32[]{:S(2)}) copy-start(f32[512,2048]{1,0:T(8,128)} %copy-done.1) | copy-start | bytes 12582916 | tf_op jit(solution)/shard_map/while/body/eval_jaxpr/while
  200.5 4.8 %copy-start.7 = (bf16[2048,128]{1,0:T(8,128)(2,1)S(1)}, bf16[2048,128]{1,0:T(8,128)(2,1)}, u32[]{:S(2)}) copy-start(bf16[2048,128]{1,0:T(8,128)(2,1)} %get-tuple-element.238) | copy-start | bytes 1572868 | tf_op jit(solution)/shard_map/while/body/eval_jaxpr/while
  213.0 1.9 copy-start.1
  215.7 4.9 %copy-start.2 = (f32[512,2048]{1,0:T(8,128)S(1)}, f32[512,2048]{1,0:T(8,128)}, u32[]{:S(2)}) copy-start(f32[512,2048]{1,0:T(8,128)} %copy-done.1) | copy-start | bytes 12582916 | tf_op jit(solution)/shard_map/while/body/eval_jaxpr/while
  215.7 4.8 %copy-start.7 = (bf16[2048,128]{1,0:T(8,128)(2,1)S(1)}, bf16[2048,128]{1,0:T(8,128)(2,1)}, u32[]{:S(2)}) copy-start(bf16[2048,128]{1,0:T(8,128)(2,1)} %get-tuple-element.238) | copy-start | bytes 1572868 | tf_op jit(solution)/shard_map/while/body/eval_jaxpr/while
  228.1 1.9 copy-start.1
  230.9 4.9 %copy-start.2 = (f32[512,2048]{1,0:T(8,128)S(1)}, f32[512,2048]{1,0:T(8,128)}, u32[]{:S(2)}) copy-start(f32[512,2048]{1,0:T(8,128)} %copy-done.1) | copy-start | bytes 12582916 | tf_op jit(solution)/shard_map/while/body/eval_jaxpr/while
  230.9 4.8 %copy-start.7 = (bf16[2048,128]{1,0:T(8,128)(2,1)S(1)}, bf16[2048,128]{1,0:T(8,128)(2,1)}, u32[]{:S(2)}) copy-start(bf16[2048,128]{1,0:T(8,128)(2,1)} %get-tuple-element.238) | copy-start | bytes 1572868 | tf_op jit(solution)/shard_map/while/body/eval_jaxpr/while
  242.2 23.1 %all-to-all-start.5 = ((bf16[16,128,128]{2,1,0:T(8,128)(2,1)}), bf16[16,128,128]{2,1,0:T(8,128)(2,1)S(1)}, u32[]{:S(2)}, u32[]{:S(2)}) async-start(bf16[16,128,128]{2,1,0:T(8,128)(2,1)} %bitcast.17), calls=%async_computation.5 | async-start | bytes 1048576 | tf_op jit(solution)/shard_map/all_to_all | solution.py:128
  284.9 19.7 %all-to-all-start.4 = ((bf16[16,128,128]{2,1,0:T(8,128)(2,1)}), bf16[16,128,128]{2,1,0:T(8,128)(2,1)S(1)}, u32[]{:S(2)}, u32[]{:S(2)}) async-start(bf16[16,128,128]{2,1,0:T(8,128)(2,1)} %bitcast.14), calls=%async_computation.4 | async-start | bytes 1048576 | tf_op jit(solution)/shard_map/all_to_all | solution.py:127
